TPU v7x, 32 devices: a whole 2x2x4 slice. The times are simulated.
32 devices in a mesh: fsdp: 8 (over y, x, core), tp: 4 (over z).
Axes of the slice: x: 2, y: 2, z: 4, core: 2. Of those that a mesh axis runs over, the one named last changes fastest.
Arguments:
- inputs: bfloat16 [16384, 1024], P(('fsdp', 'tp')), may hold values from -6 to 6
- seq_lengths: int32 [8, 7], P('fsdp'), may hold values from 1 to 512, 2048 in all within a row
- qkv_w: bfloat16 [3, 1024, 1024], P(None, 'fsdp', 'tp'), may hold values from -0.1875 to 0.1875
- out_w: bfloat16 [1024, 1024], P('tp', 'fsdp'), may hold values from -1 to 1
- fc_w: bfloat16 [1024, 4096], P('fsdp', 'tp'), may hold values from -0.1875 to 0.1875
- proj_w: bfloat16 [4096, 1024], P('tp', 'fsdp'), may hold values from -0.125 to 0.125
- ln1_gain: bfloat16 [1024], P(('fsdp', 'tp')), may hold values from 0.099609375 to 1.8984375
- ln1_bias: bfloat16 [1024], P(('fsdp', 'tp')), may hold values from -1.1953125 to 1.1953125
- q_bias: bfloat16 [1024], P(('fsdp', 'tp')), may hold values from -3 to 3
- v_bias: bfloat16 [1024], P(('fsdp', 'tp')), may hold values from -0.29882812 to 0.29882812
- out_bias: bfloat16 [1024], P(('fsdp', 'tp')), may hold values from -1.796875 to 1.796875
- ln2_gain: bfloat16 [1024], P(('fsdp', 'tp')), may hold values from 0.099609375 to 1.8984375
- ln2_bias: bfloat16 [1024], P(('fsdp', 'tp')), may hold values from -1.1953125 to 1.1953125
- fc_bias: bfloat16 [4096], P(('fsdp', 'tp')), may hold values from -1.796875 to 1.796875
- proj_bias: bfloat16 [1024], P(('fsdp', 'tp')), may hold values from -1.796875 to 1.796875
- cotangent: bfloat16 [16384, 1024], P(('fsdp', 'tp')), may hold values from -6 to 6
Outputs:
- outputs: float32 [16384, 1024], P(('fsdp', 'tp'))
- dinputs: float32 [16384, 1024], P(('fsdp', 'tp'))
- dqkv_w: float32 [3, 1024, 1024], P(None, 'fsdp', 'tp')
- dout_w: float32 [1024, 1024], P('tp', 'fsdp')
- dfc_w: float32 [1024, 4096], P('fsdp', 'tp')
- dproj_w: float32 [4096, 1024], P('tp', 'fsdp')
- dln1_gain: float32 [1024], P(('fsdp', 'tp'))
- dln1_bias: float32 [1024], P(('fsdp', 'tp'))
- dq_bias: float32 [1024], P(('fsdp', 'tp'))
- dv_bias: float32 [1024], P(('fsdp', 'tp'))
- dout_bias: float32 [1024], P(('fsdp', 'tp'))
- dln2_gain: float32 [1024], P(('fsdp', 'tp'))
- dln2_bias: float32 [1024], P(('fsdp', 'tp'))
- dfc_bias: float32 [4096], P(('fsdp', 'tp'))
- dproj_bias: float32 [1024], P(('fsdp', 'tp'))
Inputs may be any that keep to these rules, and one draw needn't show every extreme that they name: `seq_lengths`: each row lists the lengths of the 7 sequences packed in order into the 2048 tokens of one packed row; they sum to 2048 and the longest is exactly 512.
All inputs are finite; a program needn't handle non-finite values.
Results may differ from a plain program's by a relative error of at most 0.014.
Values may be sent and summed in bfloat16 or wider, within the bound.
No kernel may reach another device: no remote copies, remote signals or barrier semaphores. Data moves between devices by JAX's collectives and lax.ppermute only.
A program may use at most 192 MiB of HBM per device.

v0:
```python
import jax
import jax.numpy as jnp
from jax import lax
from jax.sharding import PartitionSpec as P

D = 1024
HD = 64
QBLK = 512


EPSILON = 1e-05
MASKED = -1e30


def layer_norm(values, gain, shift):
    center = jnp.mean(values, axis=-1, keepdims=True)
    offset = values - center
    spread = jnp.mean(offset * offset, axis=-1, keepdims=True)
    return offset * lax.rsqrt(spread + EPSILON) * gain + shift


def gelu(values):
    return jax.nn.gelu(values, approximate=True)


def segment_of(lengths, count):
    ends = jnp.cumsum(lengths)
    places = jnp.arange(count, dtype=jnp.int32)
    return jnp.sum((places[:, None] >= ends[None, :]).astype(jnp.int32), axis=1)


def place_slab(slab_values, index, length):
    return lax.dynamic_update_slice_in_dim(
        jnp.zeros((length,), jnp.float32), slab_values, index * slab_values.shape[0], 0
    )


def gather_rows(local):
    return lax.all_gather(local, "tp", axis=0, tiled=True)


def gather_grads(local):
    return lax.all_gather(local, "tp", axis=0, tiled=True)


def scatter_rows(left, right):

    def term(start, count):
        return jnp.dot(left, right, preferred_element_type=jnp.float32)

    return lax.psum_scatter(
        term(jnp.int32(0), left.shape[0] // lax.axis_size("tp") * lax.axis_size("tp")),
        "tp",
        scatter_dimension=0,
        tiled=True,
    )


def scatter_back(form, left, right):

    def term(start, count):
        return jnp.einsum(form, left, right, preferred_element_type=jnp.float32)

    return lax.psum_scatter(
        term(jnp.int32(0), left.shape[0] // lax.axis_size("tp") * lax.axis_size("tp")),
        "tp",
        scatter_dimension=0,
        tiled=True,
    )


def widen_mlp(fc_part, proj_part):
    return (
        lax.all_gather(fc_part, "tp", axis=1, tiled=True),
        lax.all_gather(proj_part, "tp", axis=0, tiled=True),
    )


def pad_front(key_rows, values, segment, block):
    zeros = jnp.zeros((block,) + key_rows.shape[1:], key_rows.dtype)
    seg_front = jnp.full((block,), -1, jnp.int32)
    return (
        jnp.concatenate([zeros, key_rows], 0),
        jnp.concatenate([zeros, values], 0),
        jnp.concatenate([seg_front, segment], 0),
    )


def block_scores(query_block, key_block, segment, seg_pad, start, block, scale):
    scores = (
        jnp.einsum("qhd,khd->hqk", query_block, key_block, preferred_element_type=jnp.float32)
        * scale
    )
    query_seg = lax.dynamic_slice_in_dim(segment, start, block, 0)
    key_seg = lax.dynamic_slice_in_dim(seg_pad, start, 2 * block, 0)
    query_place = start + jnp.arange(block, dtype=jnp.int32)
    key_place = start - block + jnp.arange(2 * block, dtype=jnp.int32)
    allowed = (key_place[None, :] <= query_place[:, None]) & (
        key_seg[None, :] == query_seg[:, None]
    )
    return jnp.where(allowed[None], scores, MASKED)


def attention_forward(queries, key_rows, values, segment, block):
    rows, heads, width = queries.shape
    scale = width ** (-0.5)
    key_pad, value_pad, seg_pad = pad_front(key_rows, values, segment, block)

    def one_block(index):
        start = index * block
        query_block = lax.dynamic_slice_in_dim(queries, start, block, 0)
        key_block = lax.dynamic_slice_in_dim(key_pad, start, 2 * block, 0)
        value_block = lax.dynamic_slice_in_dim(value_pad, start, 2 * block, 0)
        scores = block_scores(query_block, key_block, segment, seg_pad, start, block, scale)
        peak = jnp.max(scores, axis=-1, keepdims=True)
        expo = jnp.exp(scores - peak)
        total = jnp.sum(expo, axis=-1, keepdims=True)
        attend = (expo / total).astype(jnp.bfloat16)
        context = jnp.einsum(
            "hqk,khd->qhd", attend, value_block, preferred_element_type=jnp.float32
        )
        return (context.astype(jnp.bfloat16), (peak + jnp.log(total))[..., 0])

    contexts, log_total = lax.map(one_block, jnp.arange(rows // block, dtype=jnp.int32))
    return (contexts.reshape(rows, heads * width), log_total)


def attention_backward(queries, key_rows, values, segment, log_total, dcontext, block):
    rows, heads, width = queries.shape
    scale = width ** (-0.5)
    key_pad, value_pad, seg_pad = pad_front(key_rows, values, segment, block)

    def one_block(index):
        start = index * block
        query_block = lax.dynamic_slice_in_dim(queries, start, block, 0)
        key_block = lax.dynamic_slice_in_dim(key_pad, start, 2 * block, 0)
        value_block = lax.dynamic_slice_in_dim(value_pad, start, 2 * block, 0)
        grad_block = lax.dynamic_slice_in_dim(dcontext, start, block, 0)
        scores = block_scores(query_block, key_block, segment, seg_pad, start, block, scale)
        attend_full = jnp.exp(scores - log_total[index][..., None])
        attend = attend_full.astype(jnp.bfloat16)
        dattend = jnp.einsum(
            "qhd,khd->hqk", grad_block, value_block, preferred_element_type=jnp.float32
        )
        dvalue = jnp.einsum("hqk,qhd->khd", attend, grad_block, preferred_element_type=jnp.float32)
        inner = jnp.sum(attend_full * dattend, axis=-1, keepdims=True)
        dscores = (attend_full * (dattend - inner)).astype(jnp.bfloat16)
        dquery = (
            jnp.einsum("hqk,khd->qhd", dscores, key_block, preferred_element_type=jnp.float32)
            * scale
        )
        dkey = (
            jnp.einsum("hqk,qhd->khd", dscores, query_block, preferred_element_type=jnp.float32)
            * scale
        )
        return (dquery, dkey[:block], dkey[block:], dvalue[:block], dvalue[block:])

    dquery, dkey_prev, dkey_own, dvalue_prev, dvalue_own = lax.map(
        one_block, jnp.arange(rows // block, dtype=jnp.int32)
    )

    def settle(earlier, own):
        later = jnp.concatenate([earlier[1:], jnp.zeros_like(earlier[:1])], 0)
        return (own + later).reshape(rows, heads * width).astype(jnp.bfloat16)

    dquery = dquery.reshape(rows, heads * width).astype(jnp.bfloat16)
    return (dquery, settle(dkey_prev, dkey_own), settle(dvalue_prev, dvalue_own))


def per_device(
    inputs,
    seq_lengths,
    qkv_w,
    out_w,
    fc_w,
    proj_w,
    ln1_gain,
    ln1_bias,
    q_bias,
    v_bias,
    out_bias,
    ln2_gain,
    ln2_bias,
    fc_bias,
    proj_bias,
    cotangent,
):
    tp_index = lax.axis_index("tp")
    local_rows = inputs.shape[0]
    rows = local_rows * lax.axis_size("tp")
    vectors = (
        lax.all_gather(ln1_gain, ("fsdp", "tp"), axis=0, tiled=True),
        lax.all_gather(ln1_bias, ("fsdp", "tp"), axis=0, tiled=True),
        lax.all_gather(q_bias, ("fsdp", "tp"), axis=0, tiled=True),
        lax.all_gather(v_bias, ("fsdp", "tp"), axis=0, tiled=True),
        lax.all_gather(out_bias, ("fsdp", "tp"), axis=0, tiled=True),
        lax.all_gather(ln2_gain, ("fsdp", "tp"), axis=0, tiled=True),
        lax.all_gather(ln2_bias, ("fsdp", "tp"), axis=0, tiled=True),
        lax.all_gather(fc_bias, ("fsdp", "tp"), axis=0, tiled=True),
        lax.all_gather(proj_bias, ("fsdp", "tp"), axis=0, tiled=True),
    )
    (
        gain_one,
        shift_one,
        query_shift,
        value_shift,
        attn_shift,
        gain_two,
        shift_two,
        hidden_shift,
        mlp_shift,
    ) = [item.astype(jnp.float32) for item in vectors]
    qkv_full, out_full, fc_full, proj_full = (
        lax.all_gather(qkv_w, "fsdp", axis=1, tiled=True),
        lax.all_gather(out_w, "fsdp", axis=1, tiled=True),
        lax.all_gather(fc_w, "fsdp", axis=0, tiled=True),
        lax.all_gather(proj_w, "fsdp", axis=1, tiled=True),
    )
    slab = qkv_full.shape[2]
    heads = slab // HD
    query_shift = lax.dynamic_slice_in_dim(query_shift, tp_index * slab, slab, 0)
    value_shift = lax.dynamic_slice_in_dim(value_shift, tp_index * slab, slab, 0)
    segment = segment_of(seq_lengths[0], rows)
    residual = inputs.astype(jnp.float32)
    first_f, pull_one = jax.vjp(layer_norm, residual, gain_one, shift_one)
    first_rows = gather_rows(first_f.astype(jnp.bfloat16))
    projected = jnp.einsum("ri,cij->rcj", first_rows, qkv_full, preferred_element_type=jnp.float32)
    queries = (projected[:, 0] + query_shift).astype(jnp.bfloat16).reshape(rows, heads, HD)
    key_rows = projected[:, 1].astype(jnp.bfloat16).reshape(rows, heads, HD)
    values = (projected[:, 2] + value_shift).astype(jnp.bfloat16).reshape(rows, heads, HD)
    context, log_total = attention_forward(queries, key_rows, values, segment, QBLK)
    middle = residual + scatter_rows(context, out_full) + attn_shift
    second_f, pull_two = jax.vjp(layer_norm, middle, gain_two, shift_two)
    second = second_f.astype(jnp.bfloat16)
    fc_whole, proj_whole = widen_mlp(fc_full, proj_full)
    pre_act = jnp.dot(second, fc_whole, preferred_element_type=jnp.float32) + hidden_shift
    hidden_f, pull_gelu = jax.vjp(gelu, pre_act)
    hidden = hidden_f.astype(jnp.bfloat16)
    mlp_out = jnp.dot(hidden, proj_whole, preferred_element_type=jnp.float32) + mlp_shift
    outputs = middle + mlp_out
    qkv_full, out_full, fc_full, proj_full = (
        lax.all_gather(qkv_w, "fsdp", axis=1, tiled=True),
        lax.all_gather(out_w, "fsdp", axis=1, tiled=True),
        lax.all_gather(fc_w, "fsdp", axis=0, tiled=True),
        lax.all_gather(proj_w, "fsdp", axis=1, tiled=True),
    )
    dproj_bias = jnp.sum(cotangent, axis=0, dtype=jnp.float32)
    fc_whole, proj_whole = widen_mlp(fc_full, proj_full)
    dhidden = jnp.einsum("ri,ji->rj", cotangent, proj_whole, preferred_element_type=jnp.float32)
    dproj_whole = jnp.einsum("rj,ri->ji", hidden, cotangent, preferred_element_type=jnp.float32)
    dpre = pull_gelu(dhidden)[0].astype(jnp.bfloat16)
    dfc_whole = jnp.einsum("ri,rj->ij", second, dpre, preferred_element_type=jnp.float32)
    dhidden_bias = jnp.sum(dpre, axis=0, dtype=jnp.float32)
    dsecond = jnp.einsum("rj,ij->ri", dpre, fc_whole, preferred_element_type=jnp.float32)
    dfc_full, dproj_full = (
        lax.psum_scatter(
            dfc_whole.astype(jnp.bfloat16), "tp", scatter_dimension=1, tiled=True
        ).astype(jnp.float32),
        lax.psum_scatter(
            dproj_whole.astype(jnp.bfloat16), "tp", scatter_dimension=0, tiled=True
        ).astype(jnp.float32),
    )
    dmiddle_norm, dgain_two, dshift_two = pull_two(dsecond)
    dmiddle = cotangent.astype(jnp.float32) + dmiddle_norm
    dattn = dmiddle.astype(jnp.bfloat16)
    dattn_bias = jnp.sum(dattn, axis=0, dtype=jnp.float32)
    dattn_rows = gather_grads(dattn)
    dout_full = jnp.einsum("rj,ri->ji", context, dattn_rows, preferred_element_type=jnp.float32)
    dcontext = jnp.einsum("ri,ji->rj", dattn_rows, out_full, preferred_element_type=jnp.float32)
    dcontext = dcontext.astype(jnp.bfloat16).reshape(rows, heads, HD)
    dqueries, dkeys, dvalues = attention_backward(
        queries, key_rows, values, segment, log_total, dcontext, QBLK
    )
    dprojected = jnp.stack([dqueries, dkeys, dvalues], axis=1)
    dqkv_full = jnp.einsum(
        "ri,rcj->cij", first_rows, dprojected, preferred_element_type=jnp.float32
    )
    dquery_bias = place_slab(jnp.sum(dqueries, axis=0, dtype=jnp.float32), tp_index, D)
    dvalue_bias = place_slab(jnp.sum(dvalues, axis=0, dtype=jnp.float32), tp_index, D)
    dfirst = scatter_back("rcj,cij->ri", dprojected, qkv_full)
    dresidual, dgain_one, dshift_one = pull_one(dfirst)
    dinputs = dmiddle + dresidual
    dqkv_w, dout_w, dfc_w, dproj_w = (
        lax.psum_scatter(dqkv_full, "fsdp", scatter_dimension=1, tiled=True),
        lax.psum_scatter(dout_full, "fsdp", scatter_dimension=1, tiled=True),
        lax.psum_scatter(dfc_full, "fsdp", scatter_dimension=0, tiled=True),
        lax.psum_scatter(dproj_full, "fsdp", scatter_dimension=1, tiled=True),
    )
    (
        dln1_gain,
        dln1_bias,
        dq_bias,
        dv_bias,
        dout_bias,
        dln2_gain,
        dln2_bias,
        dfc_bias,
        dproj_part,
    ) = (
        lax.psum_scatter(dgain_one, ("fsdp", "tp"), scatter_dimension=0, tiled=True),
        lax.psum_scatter(dshift_one, ("fsdp", "tp"), scatter_dimension=0, tiled=True),
        lax.psum_scatter(dquery_bias, ("fsdp", "tp"), scatter_dimension=0, tiled=True),
        lax.psum_scatter(dvalue_bias, ("fsdp", "tp"), scatter_dimension=0, tiled=True),
        lax.psum_scatter(dattn_bias, ("fsdp", "tp"), scatter_dimension=0, tiled=True),
        lax.psum_scatter(dgain_two, ("fsdp", "tp"), scatter_dimension=0, tiled=True),
        lax.psum_scatter(dshift_two, ("fsdp", "tp"), scatter_dimension=0, tiled=True),
        lax.psum_scatter(dhidden_bias, ("fsdp", "tp"), scatter_dimension=0, tiled=True),
        lax.psum_scatter(dproj_bias, ("fsdp", "tp"), scatter_dimension=0, tiled=True),
    )
    return (
        outputs,
        dinputs,
        dqkv_w,
        dout_w,
        dfc_w,
        dproj_w,
        dln1_gain,
        dln1_bias,
        dq_bias,
        dv_bias,
        dout_bias,
        dln2_gain,
        dln2_bias,
        dfc_bias,
        dproj_part,
    )


def solution(mesh):
    return jax.shard_map(
        per_device,
        mesh=mesh,
        in_specs=(
            P(("fsdp", "tp"), None),
            P("fsdp", None),
            P(None, "fsdp", "tp"),
            P("tp", "fsdp"),
            P("fsdp", "tp"),
            P("tp", "fsdp"),
            P(("fsdp", "tp")),
            P(("fsdp", "tp")),
            P(("fsdp", "tp")),
            P(("fsdp", "tp")),
            P(("fsdp", "tp")),
            P(("fsdp", "tp")),
            P(("fsdp", "tp")),
            P(("fsdp", "tp")),
            P(("fsdp", "tp")),
            P(("fsdp", "tp"), None),
        ),
        out_specs=(
            P(("fsdp", "tp"), None),
            P(("fsdp", "tp"), None),
            P(None, "fsdp", "tp"),
            P("tp", "fsdp"),
            P("fsdp", "tp"),
            P("tp", "fsdp"),
            P(("fsdp", "tp")),
            P(("fsdp", "tp")),
            P(("fsdp", "tp")),
            P(("fsdp", "tp")),
            P(("fsdp", "tp")),
            P(("fsdp", "tp")),
            P(("fsdp", "tp")),
            P(("fsdp", "tp")),
            P(("fsdp", "tp")),
        ),
        check_vma=False,
    )
```

profile of v0, /device:TPU:0, one launch (start us, length us, event | category | flops | bytes accessed | tf_op | source)
XLA Modules:
  0.0 1404.0 jit_solution(10177422905579923878)
XLA Ops:
  15.8 42.2 %all-reduce.23 = (bf16[1024]{0:T(1024)(128)(2,1)S(1)}, bf16[1024]{0:T(1024)(128)(2,1)S(1)}, bf16[1024]{0:T(1024)(128)(2,1)S(1)}, bf16[1024]{0:T(1024)(128)(2,1)S...) all-reduce(bf16[1024]{0:T(1024)(128)(2,1)S(1)} %dynamic-update-slic, ...), channel_id=1, replica_groups=mesh['fsdp'=8,'tp'=4] {'fsdp','tp'}, use_global_device_ids=true, to_apply=%add.7 | all-reduce | flops 8192 | bytes 32768
  63.5 12.4 all_gather.63
  76.0 66.7 %all-gather.9.cloned.1.call-done = bf16[2048,1024]{1,0:T(8,128)(2,1)} async-done(((bf16[512,1024]{1,0:T(8,128)(2,1)}), bf16[2048,1024]{1,0:T(8,128)(2,1)}) %all-gather.9.cloned.1.call-update) | async-done | bytes 4194320 | tf_op jit(solution)/shard_map/all_gather | solution.py:39
  150.8 41.0 %while.34 = (s32[]{:T(128)}, bf16[4,512,4,64]{1,3,2,0:T(8,128)(2,1)}, f32[4,4,512]{2,1,0:T(4,128)S(1)}, s32[4]{0:T(128)S(1)}, bf16[2560,4,64]{0,2,1:T(8,128)(2,1...) while((s32[]{:T(128)}, ...), condition=%wide.region_7.8_spmd, body=%wide.region_4.7_spmd.sunk | while | flops 563740160 | bytes 28932376 | solution.py:124
  201.3 69.5 %all-gather = bf16[32,1,128]{2,1,0:T(2,128)(2,1)S(1)} all-gather(bf16[1,1,128]{2,1,0:T(2,128)(2,1)S(1)} %bitcast.114), channel_id=1, replica_groups=mesh['fsdp'=8,'tp'=4] {'fsdp','tp'}, dimensions={0}, use_global_device_ids=true | all-gather | bytes 8448 | tf_op jit(solution)/shard_map/all_gather | solution.py:199
  270.8 77.3 %reduce-scatter.9.cloned.1.call-done = f32[512,1024]{1,0:T(8,128)} async-done(((f32[2048,1024]{1,0:T(8,128)}), f32[512,1024]{1,0:T(8,128)}) %reduce-scatter.9.cloned.1.call-update) | async-done | bytes 2097168 | tf_op jit(solution)/shard_map/reduce_scatter | solution.py:51
  351.7 148.2 %all-gather.15.cloned.1.call-done = bf16[1024,4096]{1,0:T(8,128)(2,1)} async-done(((bf16[1024,1024]{1,0:T(8,128)(2,1)}), bf16[1024,4096]{1,0:T(8,128)(2,1)}) %all-gather.15.cloned.1.call-update) | async-done | bytes 8388624 | tf_op jit(solution)/shard_map/all_gather | solution.py:74
  499.9 12.2 fusion.74
  512.1 137.2 %all-gather.19.cloned.1.call-done = bf16[4096,1024]{1,0:T(8,128)(2,1)} async-done(((bf16[1024,1024]{1,0:T(8,128)(2,1)}), bf16[4096,1024]{1,0:T(8,128)(2,1)}) %all-gather.19.cloned.1.call-update) | async-done | bytes 8388624 | tf_op jit(solution)/shard_map/all_gather | solution.py:75
  649.3 16.2 %convert_reduce_fusion = (f32[4096]{0:T(1024)}, bf16[512,4096]{1,0:T(8,128)(2,1)}) fusion(f32[512,4096]{1,0:T(8,128)} %fusion.74, f32[4096]{0:T(1024)S(1)} %bitcast.111, bf16[512,1024]{1,0:T(8,128)(2,1)S(1)} %copy-done.10, bf16[4096,1024]{1,0:T(8,128)(2,1)} %all-gather.19.cloned.1.call-done), kind=kOutput, calls=%fused_computation.70 | convolution fusion | flops 4343197696 | bytes 22052864 | tf_op jit(solution)/shard_map/ri,ji->rj/dot_general | solution.py:249
  665.5 8.1 multiply_reduce_fusion.1
  676.8 10.8 convolution_convert_fusion.1
  687.7 13.0 convolution_convert_fusion
  700.8 54.9 %all-gather.21.cloned.1.call-done = bf16[2048,1024]{1,0:T(8,128)(2,1)} async-done(((bf16[512,1024]{1,0:T(8,128)(2,1)}), bf16[2048,1024]{1,0:T(8,128)(2,1)}) %all-gather.21.cloned.1.call-update) | async-done | bytes 4194320 | tf_op jit(solution)/shard_map/all_gather | solution.py:43
  760.3 71.4 %while.35 = (s32[]{:T(128)}, bf16[4,512,4,64]{1,3,2,0:T(8,128)(2,1)S(1)}, f32[4,512,4,64]{1,3,2,0:T(8,128)}, f32[4,512,4,64]{1,3,2,0:T(8,128)}, f32[4,512,4,64]{...) while((s32[]{:T(128)}, ...), condition=%wide.region_15.16_spmd, body=%wide.region_13.15_spmd.sunk | while | flops 1375600128 | bytes 78731664 | solution.py:158
  865.6 7.0 convolution_bitcast_fusion
  878.3 22.8 %reduce-scatter.17.cloned.1.call-done = bf16[1024,1024]{1,0:T(8,128)(2,1)} async-done(((bf16[1024,4096]{1,0:T(8,128)(2,1)}), bf16[1024,1024]{1,0:T(8,128)(2,1)}) %reduce-scatter.17.cloned.1.call-update) | async-done | bytes 2097168 | tf_op jit(solution)/shard_map/reduce_scatter | solution.py:256
  905.2 143.4 %reduce-scatter.21.cloned.1.call-done = bf16[1024,1024]{1,0:T(8,128)(2,1)} async-done(((bf16[4096,1024]{1,0:T(8,128)(2,1)}), bf16[1024,1024]{1,0:T(8,128)(2,1)}) %reduce-scatter.21.cloned.1.call-update) | async-done | bytes 2097168 | tf_op jit(solution)/shard_map/reduce_scatter | solution.py:259
  1054.2 13.0 add_add_fusion.3
  1068.0 30.9 %reduce-scatter.13.cloned.1.call-done = f32[3,128,256]{1,2,0:T(8,128)} async-done(((f32[3,1024,256]{1,2,0:T(8,128)}), f32[3,128,256]{1,2,0:T(8,128)}) %reduce-scatter.13.cloned.1.call-update) | async-done | bytes 393232 | tf_op jit(solution)/shard_map/reduce_scatter | solution.py:284
  1100.8 144.9 %reduce-scatter.11.cloned.1.call-done = f32[512,1024]{1,0:T(8,128)} async-done(((f32[2048,1024]{1,0:T(8,128)}), f32[512,1024]{1,0:T(8,128)}) %reduce-scatter.11.cloned.1.call-update) | async-done | bytes 2097168 | tf_op jit(solution)/shard_map/reduce_scatter | solution.py:64
  1252.1 41.8 %all-reduce.22 = (f32[1024]{0:T(1024)S(1)}, f32[1024]{0:T(1024)S(1)}, f32[1024]{0:T(1024)S(1)}, f32[1024]{0:T(1024)S(1)}, f32[1024]{0:T(1024)S(1)}, /*index=5*/f...) all-reduce(f32[1024]{0:T(1024)S(1)} %get-tuple-element.375, ...), channel_id=10, replica_groups=mesh['fsdp'=8,'tp'=4] {'fsdp','tp'}, use_global_device_ids=true, to_apply=%region_26.27.clone | all-reduce | flops 12288 | bytes 98304
  1299.1 43.0 %reduce-scatter.19.cloned.1.call-done = f32[128,1024]{1,0:T(8,128)} async-done(((f32[1024,1024]{1,0:T(8,128)}), f32[128,1024]{1,0:T(8,128)}) %reduce-scatter.19.cloned.1.call-update) | async-done | bytes 524304 | tf_op jit(solution)/shard_map/reduce_scatter | solution.py:286
  1342.2 55.1 %reduce-scatter.23.cloned.1.call-done = f32[1024,128]{1,0:T(8,128)} async-done(((f32[1024,1024]{1,0:T(8,128)}), f32[1024,128]{1,0:T(8,128)}) %reduce-scatter.23.cloned.1.call-update) | async-done | bytes 524304 | tf_op jit(solution)/shard_map/reduce_scatter | solution.py:287
  (318 shorter events, 204.9 us)
Async XLA Ops:
  7.2 52.4 %copy-start = (bf16[512,1024]{1,0:T(8,128)(2,1)S(1)}, bf16[512,1024]{1,0:T(8,128)(2,1)}, u32[]{:S(2)}) copy-start(bf16[512,1024]{1,0:T(8,128)(2,1)} %param.20) | copy-start | bytes 3145732
  7.2 68.8 %all-gather.11.cloned.1.call-start = ((), (), s32[]{:S(2)}) async-start(), calls=%async_computation.9 | async-start | bytes 1769472 | tf_op jit(solution)/shard_map/all_gather | solution.py:214
  9.1 133.7 %all-gather.9.cloned.1.call-start = ((), (), s32[]{:S(2)}) async-start(), calls=%async_computation.8 | async-start | bytes 5242880 | tf_op jit(solution)/shard_map/all_gather | solution.py:39
  61.5 138.3 %all-gather.13.cloned.1.call-start = ((), (), s32[]{:S(2)}) async-start(), calls=%async_computation.11 | async-start | bytes 2359296 | tf_op jit(solution)/shard_map/all_gather | solution.py:216
  62.3 138.9 %all-gather.17.cloned.1.call-start = ((), (), s32[]{:S(2)}) async-start(), calls=%async_computation.13 | async-start | bytes 2359296 | tf_op jit(solution)/shard_map/all_gather | solution.py:217
  62.9 285.2 %reduce-scatter.9.cloned.1.call-start = ((), (), s32[]{:S(2)}) async-start(), calls=%async_computation.10 | async-start | bytes 10485760 | tf_op jit(solution)/shard_map/reduce_scatter | solution.py:51
  199.8 300.1 %all-gather.15.cloned.1.call-start = ((), (), s32[]{:S(2)}) async-start(), calls=%async_computation.12 | async-start | bytes 10485760 | tf_op jit(solution)/shard_map/all_gather | solution.py:74
  200.4 449.0 %all-gather.19.cloned.1.call-start = ((), (), s32[]{:S(2)}) async-start(), calls=%async_computation.14 | async-start | bytes 10485760 | tf_op jit(solution)/shard_map/all_gather | solution.py:75
  201.2 554.6 %all-gather.21.cloned.1.call-start = ((), (), s32[]{:S(2)}) async-start(), calls=%async_computation.15 | async-start | bytes 5242880 | tf_op jit(solution)/shard_map/all_gather | solution.py:43
  351.7 297.6 %copy-start.10 = (bf16[512,1024]{1,0:T(8,128)(2,1)S(1)}, bf16[512,1024]{1,0:T(8,128)(2,1)}, u32[]{:S(2)}) copy-start(bf16[512,1024]{1,0:T(8,128)(2,1)} %param.35) | copy-start | bytes 3145732
  649.3 16.2 %copy-start.37 = (bf16[1024,4096]{1,0:T(8,128)(2,1)S(1)}, bf16[1024,4096]{1,0:T(8,128)(2,1)}, u32[]{:S(2)}) copy-start(bf16[1024,4096]{1,0:T(8,128)(2,1)} %all-gather.15.cloned.1.call-done) | copy-start | bytes 25165828
  676.6 224.6 %reduce-scatter.17.cloned.1.call-start = ((), (), s32[]{:S(2)}) async-start(), calls=%async_computation.19 | async-start | bytes 10485760 | tf_op jit(solution)/shard_map/reduce_scatter | solution.py:256
  687.6 361.0 %reduce-scatter.21.cloned.1.call-start = ((), (), s32[]{:S(2)}) async-start(), calls=%async_computation.21 | async-start | bytes 10485760 | tf_op jit(solution)/shard_map/reduce_scatter | solution.py:259
  700.8 59.6 %copy-start.12 = (bf16[4,512,4,64]{1,3,2,0:T(8,128)(2,1)S(1)}, bf16[4,512,4,64]{1,3,2,0:T(8,128)(2,1)}, u32[]{:S(2)}) copy-start(bf16[4,512,4,64]{1,3,2,0:T(8,128)(2,1)} %custom-call.3) | copy-start | bytes 3145732
  700.8 398.1 %reduce-scatter.13.cloned.1.call-start = ((), (), s32[]{:S(2)}) async-start(), calls=%async_computation.17 | async-start | bytes 3538944 | tf_op jit(solution)/shard_map/reduce_scatter | solution.py:284
  863.7 382.0 %reduce-scatter.11.cloned.1.call-start = ((), (), s32[]{:S(2)}) async-start(), calls=%async_computation.16 | async-start | bytes 10485760 | tf_op jit(solution)/shard_map/reduce_scatter | solution.py:64
  872.6 426.5 %reduce-scatter.15.cloned.1.call-start = ((), (), s32[]{:S(2)}) async-start(), calls=%async_computation.18 | async-start | bytes 1179648 | tf_op jit(solution)/shard_map/reduce_scatter | solution.py:285
  878.3 463.9 %reduce-scatter.19.cloned.1.call-start = ((), (), s32[]{:S(2)}) async-start(), calls=%async_computation.20 | async-start | bytes 4718592 | tf_op jit(solution)/shard_map/reduce_scatter | solution.py:286
  905.2 492.1 %reduce-scatter.23.cloned.1.call-start = ((), (), s32[]{:S(2)}) async-start(), calls=%async_computation.22 | async-start | bytes 4718592 | tf_op jit(solution)/shard_map/reduce_scatter | solution.py:287
  1054.2 191.6 %copy-start.1 = (bf16[512,1024]{1,0:T(8,128)(2,1)S(1)}, bf16[512,1024]{1,0:T(8,128)(2,1)}, u32[]{:S(2)}) copy-start(bf16[512,1024]{1,0:T(8,128)(2,1)} %param.20) | copy-start | bytes 3145732
  1054.2 191.6 %copy-start.21 = (f32[1024]{0:T(1024)S(1)}, f32[1024]{0:T(1024)}, u32[]{:S(2)}) copy-start(f32[1024]{0:T(1024)} %copy-done.20) | copy-start | bytes 12292
  1054.2 191.6 %copy-start.23 = (f32[512]{0:T(512)S(1)}, f32[512]{0:T(512)}, u32[]{:S(2)}) copy-start(f32[512]{0:T(512)} %copy-done.22) | copy-start | bytes 6148
  1067.3 180.8 %copy-start.30 = (f32[512]{0:T(512)S(1)}, f32[512]{0:T(512)}, u32[]{:S(2)}) copy-start(f32[512]{0:T(512)} %copy-done.29) | copy-start | bytes 6148
  1067.3 180.8 %copy-start.26 = (f32[512]{0:T(512)S(1)}, f32[512]{0:T(512)}, u32[]{:S(2)}) copy-start(f32[512]{0:T(512)} %copy-done.25) | copy-start | bytes 6148
  (34 other events, 108.0 us)
Sparse Core Ops, SparseCore 0:
  10.5 29.0 all-gather.10
  61.7 81.0 all-gather.8
  144.7 26.4 all-gather.12
  172.8 28.2 all-gather.16
  203.3 144.7 reduce-scatter.8
  349.5 150.3 all-gather.14
  501.5 147.8 all-gather.18
  676.7 78.9 all-gather.20
  758.1 143.0 reduce-scatter.16
  903.3 145.1 reduce-scatter.20
  1052.0 46.9 reduce-scatter.12
  1101.3 144.4 reduce-scatter.10
  1249.8 36.7 reduce-scatter.14
  1290.8 51.3 reduce-scatter.18
  1346.0 51.2 reduce-scatter.22
where the time goes:
time: 1410 us; the launch traced here: 1400 us
  waiting for transfers between devices  927 us (66%)
  matrix products  169 us (12%)
  blocking collectives  166 us (12%)
  local copies, waits for them, and re-layouts  62.5 us (4%)
  other arithmetic  50 us (4%)
  between operations  14.7 us (1%)
    all_gather x1, waiting for transfers between devices, widen_mlp(): lax.all_gather(fc_part, 'tp', axis=1, tiled=True)  148 us
    reduce_scatter x1, waiting for transfers between devices, scatter_back(): lax.psum_scatter(term(jnp.int32(0), left.shape[0] // lax.axis_size('tp')...  145 us
    reduce_scatter x1, waiting for transfers between devices, per_device(): lax.psum_scatter(dproj_whole.astype(jnp.bfloat16), 'tp', scatter_dimensio...  143 us
    all_gather x1, waiting for transfers between devices, widen_mlp(): lax.all_gather(proj_part, 'tp', axis=0, tiled=True)  137 us
    unnamed x2, blocking collectives  84 us
    reduce_scatter x1, waiting for transfers between devices, scatter_rows(): lax.psum_scatter(term(jnp.int32(0), left.shape[0] // lax.axis_size('tp')...  77.3 us
    all_gather x1, blocking collectives, per_device(): lax.all_gather(fc_bias, ('fsdp', 'tp'), axis=0, tiled=True)  69.5 us
    all_gather x1, waiting for transfers between devices, gather_rows(): return lax.all_gather(local, 'tp', axis=0, tiled=True)  66.7 us
  transfers between devices with their start and end apart: 15, of which 12 were waited for; matrix products, arithmetic and copies ran while one was open for 17% of the time, Pallas kernels for 0%

commit v1 on v0

v1 whole, which is shorter than its diff:
```python
from functools import partial

import jax
import jax.numpy as jnp
from jax import lax
from jax.experimental import pallas as pl
from jax.experimental.pallas import tpu as pltpu
from jax.sharding import PartitionSpec as P

HD = 64
QT = 256
EPSILON = 1e-05
MASKED = -1e30
BF = jnp.bfloat16
F32 = jnp.float32


def layer_norm(values, gain, shift):
    center = jnp.mean(values, axis=-1, keepdims=True)
    offset = values - center
    spread = jnp.mean(offset * offset, axis=-1, keepdims=True)
    return offset * lax.rsqrt(spread + EPSILON) * gain + shift


def gelu(values):
    return jax.nn.gelu(values, approximate=True)


def exchange(item, axis, mask):
    size = lax.axis_size(axis)
    return lax.ppermute(item, axis, [(i, i ^ mask) for i in range(size)])


def exchange_by_core(item, even_mask, odd_mask):
    size = lax.axis_size("fsdp")
    pairs = [(i, i ^ (odd_mask if i % 2 else even_mask)) for i in range(size)]
    return lax.ppermute(item, "fsdp", pairs)


def rotate(item, step):
    size = lax.axis_size("tp")
    return lax.ppermute(item, "tp", [(i, (i + step) % size) for i in range(size)])


def step_masks():
    bits = [1 << b for b in range(1, lax.axis_size("fsdp").bit_length() - 1)]
    return list(zip(bits, bits[::-1]))


def held_offsets():
    held = [(0, 0)]
    for even, odd in step_masks():
        held = held + [(a ^ even, b ^ odd) for a, b in held]
    return held


def absolute(offsets):
    mine = lax.axis_index("fsdp")
    return mine ^ jnp.where(mine % 2 == 0, offsets[0], offsets[1])


def gather_tp(part):
    size = lax.axis_size("tp")
    mine = lax.axis_index("tp")
    got = [part] + [rotate(part, k) for k in range(1, size)]
    return jnp.concatenate(
        [lax.select_n((mine - p) % size, *got) for p in range(size)], axis=-1
    )


def gather_weight(part):
    slab = gather_tp(part)
    held = [(slab, 0, 0)]
    for even, odd in step_masks():
        held = held + [
            (exchange_by_core(item, even, odd), a ^ even, b ^ odd) for item, a, b in held
        ]
    held = held + [(exchange(item, "fsdp", 1), b ^ 1, a ^ 1) for item, a, b in held]
    count = lax.axis_size("fsdp")
    n, rows, cols = slab.shape
    whole = jnp.zeros((n, count, rows, cols), part.dtype)
    for item, a, b in held:
        whole = lax.dynamic_update_slice(
            whole, item[:, None], (0, absolute((a, b)), 0, 0)
        )
    return whole.reshape(n, count * rows, cols)


def scatter_weight(grad):
    count = lax.axis_size("fsdp")
    size = lax.axis_size("tp")
    n, all_rows, all_cols = grad.shape
    rows, cols = all_rows // count, all_cols // size
    blocks = grad.reshape(n, count, rows, all_cols)

    def block(offsets):
        return lax.dynamic_slice(
            blocks, (0, absolute(offsets), 0, 0), (n, 1, rows, all_cols)
        )[:, 0]

    held = {}
    for a, b in held_offsets():
        got = exchange(block((a ^ 1, b ^ 1)), "fsdp", 1)
        held[(a, b)] = got
    mixed = {}
    for a, b in held_offsets():
        mixed[(a, b)] = (block((a, b)).astype(F32) + held[(b, a)].astype(F32)).astype(BF)
    held = mixed
    for even, odd in step_masks()[::-1]:
        keep = list(held)[: len(held) // 2]
        held = {
            (a, b): (
                held[(a, b)].astype(F32)
                + exchange_by_core(held[(a ^ even, b ^ odd)], even, odd).astype(F32)
            ).astype(BF)
            for a, b in keep
        }
    slab = held[(0, 0)]
    mine = lax.axis_index("tp")
    parts = [slab[:, :, p * cols : (p + 1) * cols] for p in range(size)]
    total = lax.select_n(mine, *parts).astype(F32)
    for k in range(1, size):
        total = total + rotate(lax.select_n((mine + k) % size, *parts), k).astype(F32)
    return total


def gather_vectors(vectors):
    pack = jnp.concatenate(vectors)[None, None]
    size = lax.axis_size("tp")
    mine = lax.axis_index("tp")
    got = [pack] + [rotate(pack, k) for k in range(1, size)]
    pack = jnp.concatenate(
        [lax.select_n((mine - p) % size, *got) for p in range(size)], axis=1
    )
    where = lax.axis_index("fsdp")
    for b in range(lax.axis_size("fsdp").bit_length() - 1):
        other = exchange(pack, "fsdp", 1 << b)
        high = (where >> b) % 2 == 1
        pack = jnp.concatenate(
            [jnp.where(high, other, pack), jnp.where(high, pack, other)], axis=0
        )
    out, at = [], 0
    for item in vectors:
        out.append(pack[:, :, at : at + item.shape[0]].reshape(-1).astype(F32))
        at += item.shape[0]
    return out


def scatter_vectors(vectors):
    count = lax.axis_size("fsdp")
    size = lax.axis_size("tp")
    pack = jnp.concatenate([v.reshape(count, size, -1) for v in vectors], axis=2)
    where = lax.axis_index("fsdp")
    for b in range(count.bit_length() - 1)[::-1]:
        half = pack.shape[0] // 2
        high = (where >> b) % 2 == 1
        low_part, high_part = pack[:half], pack[half:]
        keep = jnp.where(high, high_part, low_part)
        send = jnp.where(high, low_part, high_part)
        pack = keep + exchange(send, "fsdp", 1 << b)
    pack = pack[0]
    mine = lax.axis_index("tp")
    rows = [pack[p] for p in range(size)]
    total = lax.select_n(mine, *rows)
    for k in range(1, size):
        total = total + rotate(lax.select_n((mine + k) % size, *rows), k)
    out, at = [], 0
    for v in vectors:
        length = v.shape[0] // (count * size)
        out.append(total[at : at + length])
        at += length
    return out


def head_lanes(shape, head):
    lane = lax.broadcasted_iota(jnp.int32, shape, 1)
    return (lane >= head * HD) & (lane < (head + 1) * HD)


def nt(left, right):
    return lax.dot_general(left, right, (((1,), (1,)), ((), ())), preferred_element_type=F32)


def nn(left, right):
    return lax.dot_general(left, right, (((1,), (0,)), ((), ())), preferred_element_type=F32)


def allowed_keys(lo_row, start, keys, queries, rows):
    key = start + lax.broadcasted_iota(jnp.int32, (keys, queries), 0)
    query = rows + start + lax.broadcasted_iota(jnp.int32, (keys, queries), 1)
    return (key >= lo_row) & (key <= query)


def attend_forward(lo_ref, q_ref, k_ref, v_ref, ctx_ref, lse_ref):
    rows = q_ref.shape[0]
    width = rows + QT
    value_t = v_ref[...].T
    for tile in range(rows // QT):
        start = tile * QT
        query = q_ref[pl.ds(start, QT), :] * jnp.asarray(HD**-0.5, BF)
        keys = k_ref[pl.ds(start, width), :]
        allowed = allowed_keys(lo_ref[:, start : start + QT], start, width, QT, rows)
        parts = []
        for head in range(2):
            query_h = jnp.where(head_lanes(query.shape, head), query, jnp.zeros_like(query))
            scores = jnp.where(allowed, nt(keys, query_h), MASKED)
            peak = jnp.max(scores, axis=0, keepdims=True)
            expo = jnp.exp(scores - peak)
            total = jnp.sum(expo, axis=0, keepdims=True)
            attend = (expo * (1.0 / total)).astype(BF)
            parts.append(
                nn(value_t[head * HD : (head + 1) * HD, start : start + width], attend)
            )
            lse_ref[0, head : head + 1, start : start + QT] = peak + jnp.log(total)
        ctx_ref[pl.ds(start, QT), :] = jnp.concatenate(parts, axis=0).T.astype(BF)


def attend_backward(
    lo_ref, q_ref, k_ref, v_ref, ctx_ref, lse_ref, grad_ref, dq_ref, dk_ref, dv_ref, dk_acc, dv_acc
):
    rows = q_ref.shape[0]
    width = rows + QT
    scale = HD**-0.5
    dk_acc[...] = jnp.zeros_like(dk_acc)
    dv_acc[...] = jnp.zeros_like(dv_acc)
    key_t = k_ref[...].T
    for tile in range(rows // QT):
        start = tile * QT
        query = q_ref[pl.ds(start, QT), :] * jnp.asarray(scale, BF)
        grad = grad_ref[pl.ds(start, QT), :]
        keys = k_ref[pl.ds(start, width), :]
        values = v_ref[pl.ds(start, width), :]
        allowed = allowed_keys(lo_ref[:, start : start + QT], start, width, QT, rows)
        inner_t = (grad.astype(F32) * ctx_ref[pl.ds(start, QT), :].astype(F32)).T
        parts = []
        dk_sum, dv_sum = None, None
        for head in range(2):
            lanes = head_lanes(query.shape, head)
            query_h = jnp.where(lanes, query, jnp.zeros_like(query))
            grad_h = jnp.where(lanes, grad, jnp.zeros_like(grad))
            scores = jnp.where(allowed, nt(keys, query_h), MASKED)
            attend = jnp.exp(scores - lse_ref[0, head : head + 1, start : start + QT])
            inner = jnp.sum(inner_t[head * HD : (head + 1) * HD, :], axis=0, keepdims=True)
            dscores = (attend * (nt(values, grad_h) - inner)).astype(BF)
            dv_part = nn(attend.astype(BF), grad_h)
            dk_part = nn(dscores, query_h)
            dv_sum = dv_part if dv_sum is None else dv_sum + dv_part
            dk_sum = dk_part if dk_sum is None else dk_sum + dk_part
            parts.append(
                nn(key_t[head * HD : (head + 1) * HD, start : start + width], dscores) * scale
            )
        dq_ref[pl.ds(start, QT), :] = jnp.concatenate(parts, axis=0).T.astype(BF)
        dk_acc[pl.ds(start, width), :] += dk_sum
        dv_acc[pl.ds(start, width), :] += dv_sum
    dk_ref[...] = dk_acc[...].astype(BF)
    dv_ref[...] = dv_acc[...].astype(BF)


LANES = 2 * HD


def columns(rows):
    return pl.BlockSpec((rows, LANES), lambda pair: (0, pair))


def attention_forward(lo, queries, key_rows, values):
    rows, width = queries.shape
    pairs = width // LANES
    return pl.pallas_call(
        attend_forward,
        grid=(pairs,),
        in_specs=[
            pl.BlockSpec((1, rows), lambda pair: (0, 0)),
            columns(rows),
            columns(2 * rows),
            columns(2 * rows),
        ],
        out_specs=[columns(rows), pl.BlockSpec((1, 2, rows), lambda pair: (pair, 0, 0))],
        out_shape=[
            jax.ShapeDtypeStruct((rows, width), BF),
            jax.ShapeDtypeStruct((pairs, 2, rows), F32),
        ],
        compiler_params=pltpu.CompilerParams(vmem_limit_bytes=48 * 2**20),
        name="attend_forward",
    )(lo, queries, key_rows, values)


def attention_backward(lo, queries, key_rows, values, context, lse, dcontext):
    rows, width = queries.shape
    pairs = width // LANES
    return pl.pallas_call(
        attend_backward,
        grid=(pairs,),
        in_specs=[
            pl.BlockSpec((1, rows), lambda pair: (0, 0)),
            columns(rows),
            columns(2 * rows),
            columns(2 * rows),
            columns(rows),
            pl.BlockSpec((1, 2, rows), lambda pair: (pair, 0, 0)),
            columns(rows),
        ],
        out_specs=[columns(rows), columns(2 * rows), columns(2 * rows)],
        out_shape=[
            jax.ShapeDtypeStruct((rows, width), BF),
            jax.ShapeDtypeStruct((2 * rows, width), BF),
            jax.ShapeDtypeStruct((2 * rows, width), BF),
        ],
        scratch_shapes=[
            pltpu.VMEM((2 * rows, LANES), F32),
            pltpu.VMEM((2 * rows, LANES), F32),
        ],
        compiler_params=pltpu.CompilerParams(vmem_limit_bytes=48 * 2**20),
        name="attend_backward",
    )(lo, queries, key_rows, values, context, lse, dcontext)


def lowest_keys(lengths, rows):
    count = lengths.shape[0]
    step = jnp.arange(count, dtype=jnp.int32)
    ends = jnp.sum(jnp.where(step[None, :] <= step[:, None], lengths[None, :], 0), axis=1)
    base = lax.axis_index("tp") * rows
    places = base + jnp.arange(rows, dtype=jnp.int32)
    begins = jnp.max(jnp.where(ends[:, None] <= places[None, :], ends[:, None], 0), axis=0)
    return (begins - base + rows).astype(jnp.int32)[None, :]


def per_device(
    inputs,
    seq_lengths,
    qkv_w,
    out_w,
    fc_w,
    proj_w,
    ln1_gain,
    ln1_bias,
    q_bias,
    v_bias,
    out_bias,
    ln2_gain,
    ln2_bias,
    fc_bias,
    proj_bias,
    cotangent,
):
    rows = inputs.shape[0]
    (
        gain_one,
        shift_one,
        query_shift,
        value_shift,
        attn_shift,
        gain_two,
        shift_two,
        hidden_shift,
        mlp_shift,
    ) = gather_vectors(
        [ln1_gain, ln1_bias, q_bias, v_bias, out_bias, ln2_gain, ln2_bias, fc_bias, proj_bias]
    )
    tp_size = lax.axis_size("tp")
    before = lax.ppermute(inputs, "tp", [(i, i + 1) for i in range(tp_size - 1)])
    qkv_full = gather_weight(qkv_w)
    out_full = gather_weight(out_w.T[None])[0]
    fc_full = gather_weight(fc_w[None])[0]
    proj_full = gather_weight(proj_w.T[None])[0]

    lo = lowest_keys(seq_lengths[0], rows)
    residual = inputs.astype(F32)
    first_f, pull_one = jax.vjp(layer_norm, residual, gain_one, shift_one)
    first = first_f.astype(BF)
    first_before = layer_norm(before.astype(F32), gain_one, shift_one).astype(BF)
    first_both = jnp.concatenate([first_before, first], axis=0)
    queries = (
        jnp.dot(first, qkv_full[0], preferred_element_type=F32) + query_shift
    ).astype(BF)
    key_rows = jnp.dot(first_both, qkv_full[1], preferred_element_type=F32).astype(BF)
    values = (
        jnp.dot(first_both, qkv_full[2], preferred_element_type=F32) + value_shift
    ).astype(BF)
    context, lse = attention_forward(lo, queries, key_rows, values)
    attn_out = jnp.einsum("rj,ij->ri", context, out_full, preferred_element_type=F32)
    middle = residual + attn_out + attn_shift
    second_f, pull_two = jax.vjp(layer_norm, middle, gain_two, shift_two)
    second = second_f.astype(BF)
    pre_act = jnp.dot(second, fc_full, preferred_element_type=F32) + hidden_shift
    hidden_f, pull_gelu = jax.vjp(gelu, pre_act)
    hidden = hidden_f.astype(BF)
    dproj_full = jnp.einsum("ri,rj->ij", cotangent, hidden, preferred_element_type=F32)
    dproj_w = scatter_weight(dproj_full.astype(BF)[None])[0].T
    dhidden = jnp.dot(cotangent, proj_full, preferred_element_type=F32)
    dpre = pull_gelu(dhidden)[0].astype(BF)
    dfc_full = jnp.einsum("ri,rj->ij", second, dpre, preferred_element_type=F32)
    dfc_w = scatter_weight(dfc_full.astype(BF)[None])[0]
    dsecond = jnp.einsum("rj,ij->ri", dpre, fc_full, preferred_element_type=F32)
    mlp_out = jnp.einsum("rj,ij->ri", hidden, proj_full, preferred_element_type=F32)
    outputs = middle + mlp_out + mlp_shift

    dmiddle_norm, dgain_two, dshift_two = pull_two(dsecond)
    dmiddle = cotangent.astype(F32) + dmiddle_norm
    dattn = dmiddle.astype(BF)
    dcontext = jnp.dot(dattn, out_full, preferred_element_type=F32).astype(BF)
    dqueries, dkeys, dvalues = attention_backward(
        lo, queries, key_rows, values, context, lse, dcontext
    )
    dqkv_full = jnp.stack(
        [
            jnp.einsum("ri,rj->ij", first, dqueries, preferred_element_type=F32).astype(BF),
            jnp.einsum("ri,rj->ij", first_both, dkeys, preferred_element_type=F32).astype(BF),
            jnp.einsum("ri,rj->ij", first_both, dvalues, preferred_element_type=F32).astype(BF),
        ]
    )
    dqkv_w = scatter_weight(dqkv_full)
    dout_full = jnp.einsum("ri,rj->ij", dattn, context, preferred_element_type=F32)
    dout_w = scatter_weight(dout_full.astype(BF)[None])[0].T

    dfirst_both = jnp.einsum(
        "rj,ij->ri", dkeys, qkv_full[1], preferred_element_type=F32
    ) + jnp.einsum("rj,ij->ri", dvalues, qkv_full[2], preferred_element_type=F32)
    dfirst_after = lax.ppermute(
        dfirst_both[:rows].astype(BF), "tp", [(i + 1, i) for i in range(tp_size - 1)]
    )
    dfirst = (
        dfirst_both[rows:]
        + jnp.einsum("rj,ij->ri", dqueries, qkv_full[0], preferred_element_type=F32)
        + dfirst_after.astype(F32)
    )
    dresidual, dgain_one, dshift_one = pull_one(dfirst)
    dinputs = dmiddle + dresidual
    vector_grads = scatter_vectors(
        [
            dgain_one,
            dshift_one,
            jnp.sum(dqueries, axis=0, dtype=F32),
            jnp.sum(dvalues, axis=0, dtype=F32),
            jnp.sum(dattn, axis=0, dtype=F32),
            dgain_two,
            dshift_two,
            jnp.sum(dpre, axis=0, dtype=F32),
            jnp.sum(cotangent, axis=0, dtype=F32),
        ]
    )
    return (outputs, dinputs, dqkv_w, dout_w, dfc_w, dproj_w, *vector_grads)


def solution(mesh):
    vector = P(("fsdp", "tp"))
    tokens = P(("fsdp", "tp"), None)
    weights = (P(None, "fsdp", "tp"), P("tp", "fsdp"), P("fsdp", "tp"), P("tp", "fsdp"))
    return jax.shard_map(
        per_device,
        mesh=mesh,
        in_specs=(tokens, P("fsdp", None), *weights, *([vector] * 9), tokens),
        out_specs=(tokens, tokens, *weights, *([vector] * 9)),
        check_vma=False,
    )
```

time: 1410 us -> 592 us (0.42)
  waiting for transfers between devices: 927 us -> 177 us
  blocking collectives: 166 us -> 0 us
  starting transfers between devices: 0.78 us -> 138 us
  matrix products: 169 us -> 99.8 us
  Pallas kernels: 0 us -> 46.1 us
    reduce_scatter x8 -> x0, waiting for transfers between devices: 517 us -> none  [the longest x1 145 us: scatter_back(): lax.psum_scatter(term(jnp.int32(0), left.shape[0] // lax.axis_size('tp')...]
    all_gather x7 -> x0, waiting for transfers between devices: 408 us -> none  [the longest x1 148 us: widen_mlp(): lax.all_gather(fc_part, 'tp', axis=1, tiled=True)]
    ppermute x0 -> x94, waiting for transfers between devices: none -> 177 us  [the longest x24 117 us: exchange_by_core(): return lax.ppermute(item, 'fsdp', pairs)]
    ppermute x0 -> x94, starting transfers between devices: none -> 138 us  [the longest x30 92.8 us: rotate(): lax.ppermute(item, 'tp', [(i, (i + step) % size) for i in range(size)])]
    unnamed x2 -> x0, blocking collectives: 84 us -> none
    all_gather x2 -> x0, blocking collectives: 82 us -> none  [the longest x1 69.5 us: per_device(): lax.all_gather(fc_bias, ('fsdp', 'tp'), axis=0, tiled=True)]
    dot_general x40 -> x18, matrix products: 169 us -> 99.8 us  [the longest x1 16.6 us: per_device(): dhidden = jnp.dot(cotangent, proj_full, preferred_element_type=F32)]
    pallas_call x0 -> x2, Pallas kernels: none -> 46.1 us  [the longest x1 25 us: attention_forward(): pl.pallas_call(attend_forward, grid=(pairs,), in_specs=[pl.BlockSpec((1,...]
  transfers between devices with their start and end apart: 15 -> 94, of which waited for: 12 -> 32; matrix products, arithmetic and copies ran while one was open for 17% -> 21% of each run, Pallas kernels for 0% -> 4%
where the time goes in v1:
time: 592 us; the launch traced here: 586 us
  waiting for transfers between devices  177 us (30%)
  starting transfers between devices  138 us (23%)
  matrix products  99.8 us (17%)
  local copies, waits for them, and re-layouts  73.6 us (12%)
  other arithmetic  49.1 us (8%)
  Pallas kernels  46.1 us (8%)
    ppermute x24, waiting for transfers between devices, exchange_by_core(): return lax.ppermute(item, 'fsdp', pairs)  117 us
    ppermute x30, starting transfers between devices, rotate(): lax.ppermute(item, 'tp', [(i, (i + step) % size) for i in range(size)])  92.8 us
    ppermute x30, waiting for transfers between devices, rotate(): lax.ppermute(item, 'tp', [(i, (i + step) % size) for i in range(size)])  43.7 us
    ppermute x24, starting transfers between devices, exchange_by_core(): return lax.ppermute(item, 'fsdp', pairs)  26.7 us
    pallas_call x1, Pallas kernels, attention_forward(): pl.pallas_call(attend_forward, grid=(pairs,), in_specs=[pl.BlockSpec((1,...  25 us
    pallas_call x1, Pallas kernels, attention_backward(): pl.pallas_call(attend_backward, grid=(pairs,), in_specs=[pl.BlockSpec((1,...  21.1 us
    dynamic_update_slice x28, local copies, waits for them, and re-layouts, gather_weight(): lax.dynamic_update_slice(whole, item[:, None], (0, absolute((a, b)), 0, 0))  19.7 us
    dot_general x1, matrix products, per_device(): dhidden = jnp.dot(cotangent, proj_full, preferred_element_type=F32)  16.6 us
  transfers between devices with their start and end apart: 94, of which 32 were waited for; matrix products, arithmetic and copies ran while one was open for 21% of the time, Pallas kernels for 4%

profile of v1, /device:TPU:0, one launch (start us, length us, event | category | flops | bytes accessed | tf_op | source)
XLA Modules:
  0.0 586.3 jit_solution(1334812742052468693)
XLA Ops:
  34.6 7.1 %collective-permute-done.18 = bf16[1,128,256]{2,1,0:T(8,128)(2,1)S(1)} collective-permute-done((bf16[1,128,256]{2,1,0:T(8,128)(2,1)S(1)}, bf16[1,128,256]{2,1,0:T(8,128)(2,1)S(1)}, u32[]{:S(2)}, u32[]{:S(2)}) %collective-permute-start.18) | collective-permute-done | bytes 65568 | tf_op jit(solution)/shard_map/ppermute | solution.py:42
  41.7 12.0 %collective-permute-start.8 = (bf16[3,128,256]{2,1,0:T(8,128)(2,1)S(1)}, bf16[3,128,256]{2,1,0:T(8,128)(2,1)S(1)}, u32[]{:S(2)}, u32[]{:S(2)}) collective-permute-start(bf16[3,128,256]{2,1,0:T(8,128)(2,1)S(1)} %copy-done.39), channel_id=1, source_target_pairs={{0,3},{1,0},{2,1},{3,2},{4,7},{5,4},{6,5},{7,6},{8,11},{9,8},{10,9... | collective-permute-start | bytes 589832 | tf_op jit(solution)/shard_map/ppermute | solution.py:42
  57.4 12.5 %collective-permute-start.39 = (bf16[1,128,1024]{2,1,0:T(8,128)(2,1)S(1)}, bf16[1,128,1024]{2,1,0:T(8,128)(2,1)S(1)}, u32[]{:S(2)}, u32[]{:S(2)}) collective-permute-start(bf16[1,128,1024]{2,1,0:T(8,128)(2,1)S(1)} %bitcast.264), channel_id=1, source_target_pairs={{0,3},{1,0},{2,1},{3,2},{4,7},{5,4},{6,5},{7,6},{8,11},{9,8},{10,9... | collective-permute-start | bytes 786440 | tf_op jit(solution)/shard_map/ppermute | solution.py:42
  74.3 16.6 %collective-permute-start.29 = (bf16[1,128,1024]{2,1,0:T(8,128)(2,1)}, bf16[1,128,1024]{2,1,0:T(8,128)(2,1)S(1)}, u32[]{:S(2)}, u32[]{:S(2)}) collective-permute-start(bf16[1,128,1024]{2,1,0:T(8,128)(2,1)} %bitcast.25), channel_id=1, source_target_pairs={{0,3},{1,0},{2,1},{3,2},{4,7},{5,4},{6,5},{7,6},{8,11},{9,8},{10,9... | collective-permute-start | bytes 786440 | tf_op jit(solution)/shard_map/ppermute | solution.py:42
  129.8 14.2 %collective-permute-done.40 = bf16[1,128,4096]{2,1,0:T(8,128)(2,1)S(1)} collective-permute-done((bf16[1,128,4096]{2,1,0:T(8,128)(2,1)S(1)}, bf16[1,128,4096]{2,1,0:T(8,128)(2,1)S(1)}, u32[]{:S(2)}, u32[]{:S(2)}) %collective-permute-start.40) | collective-permute-done | bytes 1048608 | tf_op jit(solution)/shard_map/ppermute | solution.py:37
  148.4 18.1 %collective-permute-done.30 = bf16[1,128,4096]{2,1,0:T(8,128)(2,1)S(1)} collective-permute-done((bf16[1,128,4096]{2,1,0:T(8,128)(2,1)S(1)}, bf16[1,128,4096]{2,1,0:T(8,128)(2,1)S(1)}, u32[]{:S(2)}, u32[]{:S(2)}) %collective-permute-start.30) | collective-permute-done | bytes 1048608 | tf_op jit(solution)/shard_map/ppermute | solution.py:37
  167.9 7.0 %collective-permute-done.11 = bf16[3,128,1024]{2,1,0:T(8,128)(2,1)S(1)} collective-permute-done((bf16[3,128,1024]{2,1,0:T(8,128)(2,1)}, bf16[3,128,1024]{2,1,0:T(8,128)(2,1)S(1)}, u32[]{:S(2)}, u32[]{:S(2)}) %collective-permute-start.11) | collective-permute-done | bytes 786464 | tf_op jit(solution)/shard_map/ppermute | solution.py:37
  178.3 11.4 %collective-permute-done.42 = bf16[1,128,4096]{2,1,0:T(8,128)(2,1)S(1)} collective-permute-done((bf16[1,128,4096]{2,1,0:T(8,128)(2,1)S(1)}, bf16[1,128,4096]{2,1,0:T(8,128)(2,1)S(1)}, u32[]{:S(2)}, u32[]{:S(2)}) %collective-permute-start.42) | collective-permute-done | bytes 1048608 | tf_op jit(solution)/shard_map/ppermute | solution.py:37
  195.9 8.6 %collective-permute-done.32 = bf16[1,128,4096]{2,1,0:T(8,128)(2,1)S(1)} collective-permute-done((bf16[1,128,4096]{2,1,0:T(8,128)(2,1)S(1)}, bf16[1,128,4096]{2,1,0:T(8,128)(2,1)S(1)}, u32[]{:S(2)}, u32[]{:S(2)}) %collective-permute-start.32) | collective-permute-done | bytes 1048608 | tf_op jit(solution)/shard_map/ppermute | solution.py:37
  216.4 25.0 %attend_forward.1 = (bf16[512,1024]{1,0:T(8,128)(2,1)S(1)}, f32[8,2,512]{2,1,0:T(2,128)S(1)}) custom-call(s32[1,512]{1,0:T(1,128)S(1)} %bitcast.235, bf16[512,1024]{1,0:T(8,128)(2,1)S(1)} %add_convert_fusion.8.q_ref, bf16[1024,1024]{1,0:T(8,128)(2,1)S(1)} %convolution_convert_fusion.6.k_ref, bf16[1024,1024]{1,0:T(8,128)(2,1)} %add_convert_fusion.v_ref), custom_call_target="tpu_custom_call" | custom-call | tf_op jit(solution)/shard_map/attend_forward/pallas_call | solution.py:269
  246.6 7.1 %fusion.69 = f32[512,4096]{1,0:T(8,128)} fusion(bf16[1024,4096]{1,0:T(8,128)(2,1)S(1)} %bitcast.245, f32[512,1024]{1,0:T(8,128)S(1)} %get-tuple-element.154, f32[1024]{0:T(1024)S(1)} %reshape.461, f32[1024]{0:T(1024)S(1)} %reshape.460, f32[512]{0:T(512)S(1)} %fusion.63, f32[512]{0:T(512)S(1)} %broadcast_multiply_fusion), kind=kOutput, calls=%fused_computation.296 | convolution fusion | flops 4297588736 | bytes 18886656 | tf_op jit(solution)/shard_map/dot_general | solution.py:385
  255.2 16.6 %convert_reduce_fusion = (f32[4096]{0:T(1024)}, bf16[512,4096]{1,0:T(8,128)(2,1)}) fusion(f32[512,4096]{1,0:T(8,128)} %fusion.69, f32[4096]{0:T(1024)S(1)} %convert.29, bf16[512,1024]{1,0:T(8,128)(2,1)S(1)} %copy-done.9, bf16[1024,4096]{1,0:T(8,128)(2,1)S(1)} %bitcast.249), kind=kOutput, calls=%fused_computation.14 | convolution fusion | flops 4343197696 | bytes 22052864 | tf_op jit(solution)/shard_map/dot_general | solution.py:390
  271.8 7.6 %multiply_reduce_fusion = (f32[1024]{0:T(1024)S(1)}, f32[512]{0:T(512)S(1)}, f32[1024]{0:T(1024)S(1)}, f32[512,1024]{1,0:T(8,128)S(1)}) fusion(f32[512,1024]{1,0:T(8,128)S(1)} %get-tuple-element.154, f32[512]{0:T(512)S(1)} %fusion.63, f32[512]{0:T(512)S(1)} %broadcast_multiply_fusion, f32[1024]{0:T(1024)S(1)} %reshape.460, ...), kind=kOutput, calls=%fused_computation.68 | convolution fusion | flops 4299159040 | bytes 16795648 | tf_op jit(solution)/shard_map/rj,ij->ri/dot_general | solution.py:394
  284.4 21.1 %attend_backward.1 = (bf16[512,1024]{1,0:T(8,128)(2,1)S(1)}, bf16[1024,1024]{1,0:T(8,128)(2,1)}, bf16[1024,1024]{1,0:T(8,128)(2,1)}) custom-call(s32[1,512]{1,0:T(1,128)S(1)} %bitcast.236, bf16[512,1024]{1,0:T(8,128)(2,1)S(1)} %add_convert_fusion.8.q_ref, bf16[1024,1024]{1,0:T(8,128)(2,1)} %copy-done, bf16[1024,1024]{1,0:T(8,128)(2,1)} %add_convert_fusion.v_ref, ...), custom_call_target="tpu_custom_call" | custom-call | tf_op jit(solution)/shard_map/attend_backward/pallas_call | solution.py:291
  319.0 7.6 %convolution_convert_fusion.1 = bf16[1024,4096]{1,0:T(8,128)(2,1)} fusion(bf16[512,4096]{1,0:T(8,128)(2,1)S(1)} %copy-done.46, f32[512,1024]{1,0:T(8,128)S(1)} %copy-done.8, f32[1024]{0:T(1024)S(1)} %reshape.461, f32[1024]{0:T(1024)S(1)} %reshape.460, f32[512]{0:T(512)S(1)} %fusion.63, f32[512]{0:T(512)S(1)} %broadcast_multiply_fusion), kind=kOutput, calls=%fused_computation.17 | convolution fusion | flops 4301783040 | bytes 14692352 | tf_op jit(solution)/shard_map/ri,rj->ij/dot_general | solution.py:392
  326.6 11.7 %convolution_convert_fusion = bf16[4096,1024]{0,1:T(8,128)(2,1)} fusion(bf16[512,1024]{1,0:T(8,128)(2,1)S(1)} %copy-done.9, f32[512,4096]{1,0:T(8,128)} %fusion.69, f32[4096]{0:T(1024)S(1)} %convert.29), kind=kOutput, calls=%fused_computation.16 | convolution fusion | flops 4320133120 | bytes 17842176 | tf_op jit(solution)/shard_map/ri,rj->ij/dot_general | solution.py:388
  338.3 10.3 %add_add_fusion.3 = f32[512,1024]{1,0:T(8,128)} fusion(f32[512,1024]{1,0:T(8,128)S(1)} %copy-done.8, bf16[1024,4096]{1,0:T(8,128)(2,1)S(1)} %bitcast.252, f32[1024]{0:T(1024)S(1)} %reshape.463, f32[512,4096]{1,0:T(8,128)} %fusion.69, f32[4096]{0:T(1024)S(1)} %convert.29), kind=kOutput, calls=%fused_computation.79 | convolution fusion | flops 4316987392 | bytes 20992000 | tf_op jit(solution)/shard_map/rj,ij->ri/dot_general | solution.py:395
  410.7 10.0 %collective-permute-start.67 = (bf16[1,128,256]{1,2,0:T(8,128)(2,1)S(1)}, bf16[1,128,256]{1,2,0:T(8,128)(2,1)}, u32[]{:S(2)}, u32[]{:S(2)}) collective-permute-start(bf16[1,128,256]{1,2,0:T(8,128)(2,1)S(1)} %select_select_fusion.21), channel_id=1, source_target_pairs={{0,3},{1,0},{2,1},{3,2},{4,7},{5,4},{6,5},{7,6},{8,11},{9,8},{10,9... | collective-permute-start | bytes 196616 | tf_op jit(solution)/shard_map/ppermute | solution.py:42
  420.7 10.0 %collective-permute-done.47 = bf16[512,1024]{1,0:T(8,128)(2,1)S(1)} collective-permute-done((bf16[512,1024]{1,0:T(8,128)(2,1)}, bf16[512,1024]{1,0:T(8,128)(2,1)S(1)}, u32[]{:S(2)}, u32[]{:S(2)}) %collective-permute-start.47) | collective-permute-done | bytes 1048608 | tf_op jit(solution)/shard_map/ppermute | solution.py:419
  475.7 7.6 %collective-permute-done.83 = bf16[1,128,4096]{2,1,0:T(8,128)(2,1)S(1)} collective-permute-done((bf16[1,128,4096]{2,1,0:T(8,128)(2,1)S(1)}, bf16[1,128,4096]{2,1,0:T(8,128)(2,1)S(1)}, u32[]{:S(2)}, u32[]{:S(2)}) %collective-permute-start.83) | collective-permute-done | bytes 1048608 | tf_op jit(solution)/shard_map/ppermute | solution.py:37
  485.5 12.5 %collective-permute-done.50 = bf16[3,128,1024]{2,1,0:T(8,128)(2,1)S(1)} collective-permute-done((bf16[3,128,1024]{2,1,0:T(8,128)(2,1)S(1)}, bf16[3,128,1024]{2,1,0:T(8,128)(2,1)S(1)}, u32[]{:S(2)}, u32[]{:S(2)}) %collective-permute-start.50) | collective-permute-done | bytes 786464 | tf_op jit(solution)/shard_map/ppermute | solution.py:37
  520.7 6.5 %collective-permute-done.56 = bf16[3,128,256]{2,1,0:T(8,128)(2,1)S(1)} collective-permute-done((bf16[3,128,256]{2,1,0:T(8,128)(2,1)S(1)}, bf16[3,128,256]{2,1,0:T(8,128)(2,1)S(1)}, u32[]{:S(2)}, u32[]{:S(2)}) %collective-permute-start.56) | collective-permute-done | bytes 196640 | tf_op jit(solution)/shard_map/ppermute | solution.py:42
  543.3 13.1 %collective-permute-done.70 = bf16[1,128,4096]{2,1,0:T(8,128)(2,1)S(1)} collective-permute-done((bf16[1,128,4096]{2,1,0:T(8,128)(2,1)S(1)}, bf16[1,128,4096]{2,1,0:T(8,128)(2,1)S(1)}, u32[]{:S(2)}, u32[]{:S(2)}) %collective-permute-start.70) | collective-permute-done | bytes 1048608 | tf_op jit(solution)/shard_map/ppermute | solution.py:37
  568.8 16.3 %collective-permute-done.76 = bf16[1,128,1024]{2,1,0:T(8,128)(2,1)S(1)} collective-permute-done((bf16[1,128,1024]{2,1,0:T(8,128)(2,1)}, bf16[1,128,1024]{2,1,0:T(8,128)(2,1)S(1)}, u32[]{:S(2)}, u32[]{:S(2)}) %collective-permute-start.76) | collective-permute-done | bytes 262176 | tf_op jit(solution)/shard_map/ppermute | solution.py:42
  (441 shorter events, 293.5 us)
Async XLA Ops:
  13.9 110.5 %collective-permute-start.16 = (bf16[512,1024]{1,0:T(8,128)(2,1)}, bf16[512,1024]{1,0:T(8,128)(2,1)S(1)}, u32[]{:S(2)}, u32[]{:S(2)}) collective-permute-start(bf16[512,1024]{1,0:T(8,128)(2,1)} %param.16), channel_id=1, source_target_pairs={{0,1},{1,2},{2,3},{4,5},{5,6},{6,7},{8,9},{9,10},{10,11},{12,13},{... | collective-permute-start | bytes 3145736 | tf_op jit(solution)/shard_map/ppermute | solution.py:361
  20.2 33.5 %collective-permute-start.19 = (bf16[1,128,256]{2,1,0:T(8,128)(2,1)S(1)}, bf16[1,128,256]{2,1,0:T(8,128)(2,1)S(1)}, u32[]{:S(2)}, u32[]{:S(2)}) collective-permute-start(bf16[1,128,256]{2,1,0:T(8,128)(2,1)S(1)} %bitcast.271), channel_id=1, source_target_pairs={{0,3},{1,0},{2,1},{3,2},{4,7},{5,4},{6,5},{7,6},{8,11},{9,8},{10,9... | collective-permute-start | bytes 196616 | tf_op jit(solution)/shard_map/ppermute | solution.py:42
  22.3 31.4 %collective-permute-start.17 = (bf16[1,128,256]{2,1,0:T(8,128)(2,1)S(1)}, bf16[1,128,256]{2,1,0:T(8,128)(2,1)S(1)}, u32[]{:S(2)}, u32[]{:S(2)}) collective-permute-start(bf16[1,128,256]{2,1,0:T(8,128)(2,1)S(1)} %bitcast.272), channel_id=1, source_target_pairs={{0,1},{1,2},{2,3},{3,0},{4,5},{5,6},{6,7},{7,4},{8,9},{9,10},{10,1... | collective-permute-start | bytes 196616 | tf_op jit(solution)/shard_map/ppermute | solution.py:42
  41.7 28.1 %collective-permute-start.8 = (bf16[3,128,256]{2,1,0:T(8,128)(2,1)S(1)}, bf16[3,128,256]{2,1,0:T(8,128)(2,1)S(1)}, u32[]{:S(2)}, u32[]{:S(2)}) collective-permute-start(bf16[3,128,256]{2,1,0:T(8,128)(2,1)S(1)} %copy-done.39), channel_id=1, source_target_pairs={{0,3},{1,0},{2,1},{3,2},{4,7},{5,4},{6,5},{7,6},{8,11},{9,8},{10,9... | collective-permute-start | bytes 589832 | tf_op jit(solution)/shard_map/ppermute | solution.py:42
  57.4 33.6 %collective-permute-start.39 = (bf16[1,128,1024]{2,1,0:T(8,128)(2,1)S(1)}, bf16[1,128,1024]{2,1,0:T(8,128)(2,1)S(1)}, u32[]{:S(2)}, u32[]{:S(2)}) collective-permute-start(bf16[1,128,1024]{2,1,0:T(8,128)(2,1)S(1)} %bitcast.264), channel_id=1, source_target_pairs={{0,3},{1,0},{2,1},{3,2},{4,7},{5,4},{6,5},{7,6},{8,11},{9,8},{10,9... | collective-permute-start | bytes 786440 | tf_op jit(solution)/shard_map/ppermute | solution.py:42
  116.7 59.6 %collective-permute-start.12 = (bf16[3,128,1024]{2,1,0:T(8,128)(2,1)S(1)}, bf16[3,128,1024]{2,1,0:T(8,128)(2,1)S(1)}, u32[]{:S(2)}, u32[]{:S(2)}) collective-permute-start(bf16[3,128,1024]{2,1,0:T(8,128)(2,1)S(1)} %pad_maximum_fusion.4), channel_id=1, source_target_pairs={{0,4},{4,0},{8,12},{12,8},{16,20},{20,16},{24,28},{28,24},{1,5},{5... | collective-permute-start | bytes 2359304 | tf_op jit(solution)/shard_map/ppermute | solution.py:31
  122.4 69.7 %collective-permute-start.43 = (bf16[1,128,4096]{2,1,0:T(8,128)(2,1)S(1)}, bf16[1,128,4096]{2,1,0:T(8,128)(2,1)S(1)}, u32[]{:S(2)}, u32[]{:S(2)}) collective-permute-start(bf16[1,128,4096]{2,1,0:T(8,128)(2,1)S(1)} %copy-done.26), channel_id=1, source_target_pairs={{0,4},{4,0},{8,12},{12,8},{16,20},{20,16},{24,28},{28,24},{1,5},{5... | collective-permute-start | bytes 3145736 | tf_op jit(solution)/shard_map/ppermute | solution.py:31
  124.4 42.1 %collective-permute-start.30 = (bf16[1,128,4096]{2,1,0:T(8,128)(2,1)S(1)}, bf16[1,128,4096]{2,1,0:T(8,128)(2,1)S(1)}, u32[]{:S(2)}, u32[]{:S(2)}) collective-permute-start(bf16[1,128,4096]{2,1,0:T(8,128)(2,1)S(1)} %copy-done.27), channel_id=1, source_target_pairs={{0,8},{4,20},{8,0},{12,28},{16,24},{20,4},{24,16},{28,12},{1,9},{5... | collective-permute-start | bytes 3145736 | tf_op jit(solution)/shard_map/ppermute | solution.py:37
  146.4 28.4 %collective-permute-start.11 = (bf16[3,128,1024]{2,1,0:T(8,128)(2,1)}, bf16[3,128,1024]{2,1,0:T(8,128)(2,1)S(1)}, u32[]{:S(2)}, u32[]{:S(2)}) collective-permute-start(bf16[3,128,1024]{2,1,0:T(8,128)(2,1)} %collective-permute-done.9), channel_id=1, source_target_pairs={{0,16},{4,12},{8,24},{12,4},{16,0},{20,28},{24,8},{28,20},{1,17},{... | collective-permute-start | bytes 2359304 | tf_op jit(solution)/shard_map/ppermute | solution.py:37
  176.3 28.3 %collective-permute-start.33 = (bf16[1,128,4096]{2,1,0:T(8,128)(2,1)S(1)}, bf16[1,128,4096]{2,1,0:T(8,128)(2,1)S(1)}, u32[]{:S(2)}, u32[]{:S(2)}) collective-permute-start(bf16[1,128,4096]{2,1,0:T(8,128)(2,1)S(1)} %copy-done.27), channel_id=1, source_target_pairs={{0,4},{4,0},{8,12},{12,8},{16,20},{20,16},{24,28},{28,24},{1,5},{5... | collective-permute-start | bytes 3145736 | tf_op jit(solution)/shard_map/ppermute | solution.py:31
  204.5 49.2 %collective-permute-start.46 = (bf16[1,128,4096]{2,1,0:T(8,128)(2,1)S(1)}, bf16[1,128,4096]{2,1,0:T(8,128)(2,1)}, u32[]{:S(2)}, u32[]{:S(2)}) collective-permute-start(bf16[1,128,4096]{2,1,0:T(8,128)(2,1)S(1)} %collective-permute-done.42), channel_id=1, source_target_pairs={{0,4},{4,0},{8,12},{12,8},{16,20},{20,16},{24,28},{28,24},{1,5},{5... | collective-permute-start | bytes 3145736 | tf_op jit(solution)/shard_map/ppermute | solution.py:31
  204.6 40.2 %collective-permute-start.36 = (bf16[1,128,4096]{2,1,0:T(8,128)(2,1)S(1)}, bf16[1,128,4096]{2,1,0:T(8,128)(2,1)}, u32[]{:S(2)}, u32[]{:S(2)}) collective-permute-start(bf16[1,128,4096]{2,1,0:T(8,128)(2,1)S(1)} %collective-permute-done.32), channel_id=1, source_target_pairs={{0,4},{4,0},{8,12},{12,8},{16,20},{20,16},{24,28},{28,24},{1,5},{5... | collective-permute-start | bytes 3145736 | tf_op jit(solution)/shard_map/ppermute | solution.py:31
  364.0 37.7 %collective-permute-start.49 = (bf16[3,128,1024]{2,1,0:T(8,128)(2,1)}, bf16[3,128,1024]{2,1,0:T(8,128)(2,1)}, u32[]{:S(2)}, u32[]{:S(2)}) collective-permute-start(bf16[3,128,1024]{2,1,0:T(8,128)(2,1)} %get-tuple-element.85), channel_id=1, source_target_pairs={{0,4},{4,0},{8,12},{12,8},{16,20},{20,16},{24,28},{28,24},{1,5},{5... | collective-permute-start | bytes 2359304 | tf_op jit(solution)/shard_map/ppermute | solution.py:31
  364.0 38.4 %collective-permute-start.52 = (bf16[3,128,1024]{2,1,0:T(8,128)(2,1)}, bf16[3,128,1024]{2,1,0:T(8,128)(2,1)}, u32[]{:S(2)}, u32[]{:S(2)}) collective-permute-start(bf16[3,128,1024]{2,1,0:T(8,128)(2,1)} %get-tuple-element.83), channel_id=1, source_target_pairs={{0,4},{4,0},{8,12},{12,8},{16,20},{20,16},{24,28},{28,24},{1,5},{5... | collective-permute-start | bytes 2359304 | tf_op jit(solution)/shard_map/ppermute | solution.py:31
  369.4 30.4 %collective-permute-start.61 = (bf16[1,128,1024]{1,2,0:T(8,128)(2,1)}, bf16[1,128,1024]{1,2,0:T(8,128)(2,1)}, u32[]{:S(2)}, u32[]{:S(2)}) collective-permute-start(bf16[1,128,1024]{1,2,0:T(8,128)(2,1)} %bitcast.266), channel_id=1, source_target_pairs={{0,4},{4,0},{8,12},{12,8},{16,20},{20,16},{24,28},{28,24},{1,5},{5... | collective-permute-start | bytes 786440 | tf_op jit(solution)/shard_map/ppermute | solution.py:31
  397.3 33.4 %collective-permute-start.47 = (bf16[512,1024]{1,0:T(8,128)(2,1)}, bf16[512,1024]{1,0:T(8,128)(2,1)S(1)}, u32[]{:S(2)}, u32[]{:S(2)}) collective-permute-start(bf16[512,1024]{1,0:T(8,128)(2,1)} %slice.412), channel_id=1, source_target_pairs={{1,0},{2,1},{3,2},{5,4},{6,5},{7,6},{9,8},{10,9},{11,10},{13,12},{... | collective-permute-start | bytes 3145736 | tf_op jit(solution)/shard_map/ppermute | solution.py:419
  400.0 54.5 %collective-permute-start.79 = (bf16[1,128,4096]{2,1,0:T(8,128)(2,1)}, bf16[1,128,4096]{2,1,0:T(8,128)(2,1)}, u32[]{:S(2)}, u32[]{:S(2)}) collective-permute-start(bf16[1,128,4096]{2,1,0:T(8,128)(2,1)} %get-tuple-element.73), channel_id=1, source_target_pairs={{0,4},{4,0},{8,12},{12,8},{16,20},{20,16},{24,28},{28,24},{1,5},{5... | collective-permute-start | bytes 3145736 | tf_op jit(solution)/shard_map/ppermute | solution.py:31
  407.3 47.7 %collective-permute-start.82 = (bf16[1,128,4096]{2,1,0:T(8,128)(2,1)}, bf16[1,128,4096]{2,1,0:T(8,128)(2,1)}, u32[]{:S(2)}, u32[]{:S(2)}) collective-permute-start(bf16[1,128,4096]{2,1,0:T(8,128)(2,1)} %get-tuple-element.71), channel_id=1, source_target_pairs={{0,4},{4,0},{8,12},{12,8},{16,20},{20,16},{24,28},{28,24},{1,5},{5... | collective-permute-start | bytes 3145736 | tf_op jit(solution)/shard_map/ppermute | solution.py:31
  410.7 36.0 %collective-permute-start.67 = (bf16[1,128,256]{1,2,0:T(8,128)(2,1)S(1)}, bf16[1,128,256]{1,2,0:T(8,128)(2,1)}, u32[]{:S(2)}, u32[]{:S(2)}) collective-permute-start(bf16[1,128,256]{1,2,0:T(8,128)(2,1)S(1)} %select_select_fusion.21), channel_id=1, source_target_pairs={{0,3},{1,0},{2,1},{3,2},{4,7},{5,4},{6,5},{7,6},{8,11},{9,8},{10,9... | collective-permute-start | bytes 196616 | tf_op jit(solution)/shard_map/ppermute | solution.py:42
  469.4 38.9 %collective-permute-start.71 = (bf16[1,128,4096]{2,1,0:T(8,128)(2,1)S(1)}, bf16[1,128,4096]{2,1,0:T(8,128)(2,1)S(1)}, u32[]{:S(2)}, u32[]{:S(2)}) collective-permute-start(bf16[1,128,4096]{2,1,0:T(8,128)(2,1)S(1)} %copy-done.21), channel_id=1, source_target_pairs={{0,4},{4,0},{8,12},{12,8},{16,20},{20,16},{24,28},{28,24},{1,5},{5... | collective-permute-start | bytes 3145736 | tf_op jit(solution)/shard_map/ppermute | solution.py:31
  473.9 39.5 %collective-permute-start.73 = (bf16[1,128,4096]{2,1,0:T(8,128)(2,1)S(1)}, bf16[1,128,4096]{2,1,0:T(8,128)(2,1)S(1)}, u32[]{:S(2)}, u32[]{:S(2)}) collective-permute-start(bf16[1,128,4096]{2,1,0:T(8,128)(2,1)S(1)} %get-tuple-element.81), channel_id=1, source_target_pairs={{0,16},{4,12},{8,24},{12,4},{16,0},{20,28},{24,8},{28,20},{1,17},{... | collective-permute-start | bytes 3145736 | tf_op jit(solution)/shard_map/ppermute | solution.py:37
  485.4 43.1 %collective-permute-start.78 = (bf16[1,128,4096]{2,1,0:T(8,128)(2,1)S(1)}, bf16[1,128,4096]{2,1,0:T(8,128)(2,1)S(1)}, u32[]{:S(2)}, u32[]{:S(2)}) collective-permute-start(bf16[1,128,4096]{2,1,0:T(8,128)(2,1)S(1)} %copy-done.20), channel_id=1, source_target_pairs={{0,4},{4,0},{8,12},{12,8},{16,20},{20,16},{24,28},{28,24},{1,5},{5... | collective-permute-start | bytes 3145736 | tf_op jit(solution)/shard_map/ppermute | solution.py:31
  498.0 37.9 %collective-permute-start.80 = (bf16[1,128,4096]{2,1,0:T(8,128)(2,1)S(1)}, bf16[1,128,4096]{2,1,0:T(8,128)(2,1)S(1)}, u32[]{:S(2)}, u32[]{:S(2)}) collective-permute-start(bf16[1,128,4096]{2,1,0:T(8,128)(2,1)S(1)} %get-tuple-element.74), channel_id=1, source_target_pairs={{0,16},{4,12},{8,24},{12,4},{16,0},{20,28},{24,8},{28,20},{1,17},{... | collective-permute-start | bytes 3145736 | tf_op jit(solution)/shard_map/ppermute | solution.py:37
  527.2 29.2 %collective-permute-start.70 = (bf16[1,128,4096]{2,1,0:T(8,128)(2,1)S(1)}, bf16[1,128,4096]{2,1,0:T(8,128)(2,1)S(1)}, u32[]{:S(2)}, u32[]{:S(2)}) collective-permute-start(bf16[1,128,4096]{2,1,0:T(8,128)(2,1)S(1)} %get-tuple-element.80), channel_id=1, source_target_pairs={{0,16},{4,12},{8,24},{12,4},{16,0},{20,28},{24,8},{28,20},{1,17},{... | collective-permute-start | bytes 3145736 | tf_op jit(solution)/shard_map/ppermute | solution.py:37
  (121 other events, 1485.5 us)
